TPU v7x, 512 devices: a whole 4x4x16 slice. The times are simulated.
512 devices in a mesh: bl: 32 (over y, x, core), dir: 16 (over z).
Axes of the slice: x: 4, y: 4, z: 16, core: 2. Of those that a mesh axis runs over, the one named last changes fastest.
Arguments:
- visibilities: float32 [8, 16, 8192], P(None, 'dir', 'bl'), may hold values from -24 to 24
- coherencies: bfloat16 [32, 8, 16, 8192], P('dir', None, None, 'bl'), may hold values from -6 to 6
- gain_offsets: float32 [32, 8, 512], P(None, None, 'bl'), may hold values from -1.5 to 1.5
- stations: int32 [2, 8192], P(None, 'bl'), may hold values from 0 to 511, as said below
- solve_order: int32 [32], replicated, may hold values from 0 to 31, each once
- counts: int32 [32], replicated, may hold values from 1 to 2
- damping: int32 [32], replicated, may hold values from 1 to 8
Outputs:
- gains: float32 [32, 8, 512], P(None, None, 'bl')
- residual: float32 [8, 16, 8192], P(None, 'dir', 'bl')
Inputs may be any that keep to these rules, and one draw needn't show every extreme that they name: Each baseline names two different stations. `solve_order`: each direction appears once.
All inputs are finite; a program needn't handle non-finite values.
Results may differ from a plain program's by a relative error of at most 0.0003.
Values may be sent and summed in bfloat16 or wider, within the bound.
A program may use at most 64 MiB of HBM per device.

v0:
```python
import jax
import jax.numpy as jnp
from jax import lax
from jax.sharding import PartitionSpec as P

LM_ITERS = 2
SOLVED = 4


def from_root(shard, axis, root):
    mine = lax.axis_index(axis) == root
    return lax.psum(jnp.where(mine, shard, jnp.zeros_like(shard)), axis)


def matrix_entry(mat, i, j):
    return (mat[4 * i + 2 * j], mat[4 * i + 2 * j + 1])


def matmul_two(left, right):
    pieces = []
    for i in (0, 1):
        for j in (0, 1):
            left_r0, left_i0 = matrix_entry(left, i, 0)
            left_r1, left_i1 = matrix_entry(left, i, 1)
            right_r0, right_i0 = matrix_entry(right, 0, j)
            right_r1, right_i1 = matrix_entry(right, 1, j)
            pieces.append(
                left_r0 * right_r0 - left_i0 * right_i0 + left_r1 * right_r1 - left_i1 * right_i1
            )
            pieces.append(
                left_r0 * right_i0 + left_i0 * right_r0 + left_r1 * right_i1 + left_i1 * right_r1
            )
    return jnp.stack(pieces)


def adjoint(mat):
    return jnp.stack([mat[0], -mat[1], mat[4], -mat[5], mat[2], -mat[3], mat[6], -mat[7]])


def apply_gains(gain_p, coher_now, gain_q):
    return matmul_two(matmul_two(gain_p, coher_now), adjoint(gain_q))


def gram_parts(gram):
    return jnp.stack([gram[0], gram[6], gram[2], gram[3]])


def station_terms(gain_p, gain_q, coher_now, target):
    z_rows = matmul_two(coher_now, adjoint(gain_q))
    y_rows = matmul_two(adjoint(coher_now), adjoint(gain_p))
    leading_endpoint = jnp.concatenate(
        [matmul_two(target, adjoint(z_rows)), gram_parts(matmul_two(z_rows, adjoint(z_rows)))], 0
    )
    second = jnp.concatenate(
        [
            matmul_two(adjoint(target), adjoint(y_rows)),
            gram_parts(matmul_two(y_rows, adjoint(y_rows))),
        ],
        0,
    )
    return (jnp.sum(leading_endpoint, axis=1), jnp.sum(second, axis=1))


def solve_station(gathered_sums, gain_now, damp_value):
    numerator = gathered_sums[:8] + damp_value * gain_now
    diag_a = gathered_sums[8] + damp_value
    diag_d = gathered_sums[9] + damp_value
    cross_r = gathered_sums[10]
    cross_i = gathered_sums[11]
    determinant = diag_a * diag_d - cross_r * cross_r - cross_i * cross_i
    zeros_row = jnp.zeros_like(determinant)
    inverse = (
        jnp.stack([diag_d, zeros_row, -cross_r, -cross_i, -cross_r, cross_i, diag_a, zeros_row])
        / determinant
    )
    return matmul_two(numerator, inverse)


def on_device(visibilities, coherencies, gain_offsets, stations, solve_order, counts, damping):
    identity = jnp.zeros((8,), jnp.float32).at[0].set(1.0).at[6].set(1.0)
    start = lax.all_gather(gain_offsets, "bl", axis=2, tiled=True) + identity[None, :, None]
    groups = lax.axis_size("bl")
    channels = visibilities.shape[1]
    total_channels = coherencies.shape[2]
    owned_count = coherencies.shape[0]
    station_count = start.shape[2]
    damping_factor = visibilities.shape[2] * groups * total_channels / station_count
    lane_index = lax.axis_index("dir")
    ends_p = jnp.take(start, stations[0], axis=2)
    ends_q = jnp.take(start, stations[1], axis=2)
    owned_p = lax.dynamic_slice_in_dim(ends_p, lane_index * owned_count, owned_count, 0)
    owned_q = lax.dynamic_slice_in_dim(ends_q, lane_index * owned_count, owned_count, 0)
    gain_p = jnp.transpose(owned_p, (1, 0, 2))[:, :, None, :]
    gain_q = jnp.transpose(owned_q, (1, 0, 2))[:, :, None, :]
    coher_owned = jnp.transpose(coherencies, (1, 0, 2, 3)).astype(jnp.float32)
    partial_value = jnp.sum(apply_gains(gain_p, coher_owned, gain_q), axis=1)
    first_model = lax.psum_scatter(partial_value, "dir", scatter_dimension=1, tiled=True)
    first_residual = visibilities - first_model

    def direction_model(gain_now, coher_now):
        gain_p = jnp.take(gain_now, stations[0], axis=1)[:, None, :]
        gain_q = jnp.take(gain_now, stations[1], axis=1)[:, None, :]
        return apply_gains(gain_p, coher_now, gain_q)

    def sweep(step_index, state):
        gain_table, residual = state
        which = solve_order[step_index]
        owner_row = lax.dynamic_index_in_dim(coherencies, which % owned_count, 0, keepdims=False)
        broadcast_rows = from_root(owner_row, "dir", which // owned_count)
        coher_now = lax.dynamic_slice_in_dim(
            broadcast_rows, lane_index * channels, channels, 1
        ).astype(jnp.float32)
        damp_value = damping[which].astype(jnp.float32) * damping_factor
        gain_start = gain_table[which]
        target = residual + direction_model(gain_start, coher_now)

        def iterate(round_index, gain_now):
            gain_p = jnp.take(gain_now, stations[0], axis=1)[:, None, :]
            gain_q = jnp.take(gain_now, stations[1], axis=1)[:, None, :]
            leading_endpoint, second = station_terms(gain_p, gain_q, coher_now, target)
            local_sums = (
                jax.ops.segment_sum(leading_endpoint.T, stations[0], station_count)
                + jax.ops.segment_sum(second.T, stations[1], station_count)
            ).T
            gathered_sums = lax.psum(local_sums, ("bl", "dir"))
            updated = solve_station(gathered_sums, gain_now, damp_value)
            return jnp.where(round_index < counts[which], updated, gain_now)

        gain_final = lax.fori_loop(0, LM_ITERS, iterate, gain_start)
        residual = target - direction_model(gain_final, coher_now)
        return (gain_table.at[which].set(gain_final), residual)

    gain_table, residual = lax.fori_loop(0, SOLVED, sweep, (start, first_residual))
    own_width = station_count // groups
    gains = lax.dynamic_slice_in_dim(gain_table, lax.axis_index("bl") * own_width, own_width, 2)
    return (gains, residual)


def solution(mesh):
    return jax.shard_map(
        on_device,
        mesh=mesh,
        in_specs=(
            P(None, "dir", "bl"),
            P("dir", None, None, "bl"),
            P(None, None, "bl"),
            P(None, "bl"),
            P(),
            P(),
            P(),
        ),
        out_specs=(P(None, None, "bl"), P(None, "dir", "bl")),
        check_vma=False,
    )
```

profile of v0, /device:TPU:1, one launch (start us, length us, event | category | flops | bytes accessed | tf_op | source)
XLA Modules:
  0.0 1577.4 jit_solution(7976615437648332978)
XLA Ops:
  9.8 29.8 %all_gather.3 = f32[32,8,512]{0,1,2:T(8,128)S(1)} all-gather(f32[32,8,16]{0,1,2:T(8,128)S(1)} %copy.1403), channel_id=1, replica_groups=mesh['bl'=32,'dir'=16] {'bl'}, dimensions={2}, use_global_device_ids=true | all-gather | bytes 540672 | tf_op jit(solution)/shard_map/all_gather | solution.py:81
  48.5 7.5 copy.1415
  56.0 49.5 %reduce-scatter.2.cloned.1.call-done = f32[8,1,256]{2,0,1:T(8,128)} async-done(((f32[8,16,256]{2,0,1:T(8,128)}), f32[8,1,256]{2,0,1:T(8,128)}) %reduce-scatter.2.cloned.1.call-update) | async-done | bytes 8208 | tf_op jit(solution)/shard_map/reduce_scatter | solution.py:97
  106.3 1457.3 %while.54 = (s32[]{:T(128)}, f32[32,8,512]{1,2,0:T(8,128)}, f32[8,1,256]{2,1,0:T(1,128)S(1)}, s32[32]{0:T(128)S(1)}, bf16[2,8,16,256]{3,2,1,0:T(8,128)(2,1)S(1)}...) while((s32[]{:T(128)}, f32[32,8,512]{1,2,0:T(8,128)}, ...), condition=%wide.region_10.13_spmd, body=%wide.region_2.12_spmd.sunk | while | flops 323119 | bytes 2925989 | solution.py:133
  116.9 125.3 %all-reduce.2.cloned.1.call-done = bf16[8,16,256]{2,1,0:T(8,128)(2,1)} async-done(((bf16[8,16,256]{2,1,0:T(8,128)(2,1)}), bf16[8,16,256]{2,1,0:T(8,128)(2,1)}) %all-reduce.2.cloned.1.call-update) | async-done | bytes 65552 | tf_op jit(solution)/shard_map/while/body/eval_jaxpr/psum | solution.py:12
  243.2 235.5 %while.55 = (s32[]{:T(128)}, f32[8,512]{0,1:T(8,128)S(1)}, s32[1]{0:T(128)}, s32[2,256]{1,0:T(2,128)S(1)}, f32[8,1,256]{2,1,0:T(1,128)S(1)}, /*index=5*/f32[8,1,...) while((s32[]{:T(128)}, f32[8,512]{0,1:T(8,128)S(1)}, ...), condition=%wide.region_9.11_spmd, body=%wide.region_5.10_spmd.sunk | while | flops 164865 | bytes 1329347 | solution.py:129
  249.5 112.0 %psum.29 = f32[12,512]{0,1:T(8,128)S(1)} all-reduce(f32[12,512]{0,1:T(8,128)S(1)} %add_bitcast_fusion.2), channel_id=1, replica_groups=mesh['bl'=32,'dir'=16] {'bl','dir'}, use_global_device_ids=true, to_apply=%region_8.9 | all-reduce | flops 6144 | bytes 49152 | tf_op jit(solution)/shard_map/while/body/eval_jaxpr/while/body/eval_jaxpr/psum | solution.py:125
  372.5 101.4 %psum.29 = f32[12,512]{0,1:T(8,128)S(1)} all-reduce(f32[12,512]{0,1:T(8,128)S(1)} %add_bitcast_fusion.2), channel_id=1, replica_groups=mesh['bl'=32,'dir'=16] {'bl','dir'}, use_global_device_ids=true, to_apply=%region_8.9 | all-reduce | flops 6144 | bytes 49152 | tf_op jit(solution)/shard_map/while/body/eval_jaxpr/while/body/eval_jaxpr/psum | solution.py:125
  480.5 2.3 fusion.153
  493.4 109.1 %all-reduce.2.cloned.1.call-done = bf16[8,16,256]{2,1,0:T(8,128)(2,1)} async-done(((bf16[8,16,256]{2,1,0:T(8,128)(2,1)}), bf16[8,16,256]{2,1,0:T(8,128)(2,1)}) %all-reduce.2.cloned.1.call-update) | async-done | bytes 65552 | tf_op jit(solution)/shard_map/while/body/eval_jaxpr/psum | solution.py:12
  603.5 235.5 %while.55 = (s32[]{:T(128)}, f32[8,512]{0,1:T(8,128)S(1)}, s32[1]{0:T(128)}, s32[2,256]{1,0:T(2,128)S(1)}, f32[8,1,256]{2,1,0:T(1,128)S(1)}, /*index=5*/f32[8,1,...) while((s32[]{:T(128)}, f32[8,512]{0,1:T(8,128)S(1)}, ...), condition=%wide.region_9.11_spmd, body=%wide.region_5.10_spmd.sunk | while | flops 164865 | bytes 1329347 | solution.py:129
  609.7 112.0 %psum.29 = f32[12,512]{0,1:T(8,128)S(1)} all-reduce(f32[12,512]{0,1:T(8,128)S(1)} %add_bitcast_fusion.2), channel_id=1, replica_groups=mesh['bl'=32,'dir'=16] {'bl','dir'}, use_global_device_ids=true, to_apply=%region_8.9 | all-reduce | flops 6144 | bytes 49152 | tf_op jit(solution)/shard_map/while/body/eval_jaxpr/while/body/eval_jaxpr/psum | solution.py:125
  732.8 101.4 %psum.29 = f32[12,512]{0,1:T(8,128)S(1)} all-reduce(f32[12,512]{0,1:T(8,128)S(1)} %add_bitcast_fusion.2), channel_id=1, replica_groups=mesh['bl'=32,'dir'=16] {'bl','dir'}, use_global_device_ids=true, to_apply=%region_8.9 | all-reduce | flops 6144 | bytes 49152 | tf_op jit(solution)/shard_map/while/body/eval_jaxpr/while/body/eval_jaxpr/psum | solution.py:125
  853.6 109.1 %all-reduce.2.cloned.1.call-done = bf16[8,16,256]{2,1,0:T(8,128)(2,1)} async-done(((bf16[8,16,256]{2,1,0:T(8,128)(2,1)}), bf16[8,16,256]{2,1,0:T(8,128)(2,1)}) %all-reduce.2.cloned.1.call-update) | async-done | bytes 65552 | tf_op jit(solution)/shard_map/while/body/eval_jaxpr/psum | solution.py:12
  963.7 235.5 %while.55 = (s32[]{:T(128)}, f32[8,512]{0,1:T(8,128)S(1)}, s32[1]{0:T(128)}, s32[2,256]{1,0:T(2,128)S(1)}, f32[8,1,256]{2,1,0:T(1,128)S(1)}, /*index=5*/f32[8,1,...) while((s32[]{:T(128)}, f32[8,512]{0,1:T(8,128)S(1)}, ...), condition=%wide.region_9.11_spmd, body=%wide.region_5.10_spmd.sunk | while | flops 164865 | bytes 1329347 | solution.py:129
  970.0 112.0 %psum.29 = f32[12,512]{0,1:T(8,128)S(1)} all-reduce(f32[12,512]{0,1:T(8,128)S(1)} %add_bitcast_fusion.2), channel_id=1, replica_groups=mesh['bl'=32,'dir'=16] {'bl','dir'}, use_global_device_ids=true, to_apply=%region_8.9 | all-reduce | flops 6144 | bytes 49152 | tf_op jit(solution)/shard_map/while/body/eval_jaxpr/while/body/eval_jaxpr/psum | solution.py:125
  1093.0 101.4 %psum.29 = f32[12,512]{0,1:T(8,128)S(1)} all-reduce(f32[12,512]{0,1:T(8,128)S(1)} %add_bitcast_fusion.2), channel_id=1, replica_groups=mesh['bl'=32,'dir'=16] {'bl','dir'}, use_global_device_ids=true, to_apply=%region_8.9 | all-reduce | flops 6144 | bytes 49152 | tf_op jit(solution)/shard_map/while/body/eval_jaxpr/while/body/eval_jaxpr/psum | solution.py:125
  1201.0 2.3 fusion.153
  1213.9 109.1 %all-reduce.2.cloned.1.call-done = bf16[8,16,256]{2,1,0:T(8,128)(2,1)} async-done(((bf16[8,16,256]{2,1,0:T(8,128)(2,1)}), bf16[8,16,256]{2,1,0:T(8,128)(2,1)}) %all-reduce.2.cloned.1.call-update) | async-done | bytes 65552 | tf_op jit(solution)/shard_map/while/body/eval_jaxpr/psum | solution.py:12
  1324.0 235.5 %while.55 = (s32[]{:T(128)}, f32[8,512]{0,1:T(8,128)S(1)}, s32[1]{0:T(128)}, s32[2,256]{1,0:T(2,128)S(1)}, f32[8,1,256]{2,1,0:T(1,128)S(1)}, /*index=5*/f32[8,1,...) while((s32[]{:T(128)}, f32[8,512]{0,1:T(8,128)S(1)}, ...), condition=%wide.region_9.11_spmd, body=%wide.region_5.10_spmd.sunk | while | flops 164865 | bytes 1329347 | solution.py:129
  1330.2 112.0 %psum.29 = f32[12,512]{0,1:T(8,128)S(1)} all-reduce(f32[12,512]{0,1:T(8,128)S(1)} %add_bitcast_fusion.2), channel_id=1, replica_groups=mesh['bl'=32,'dir'=16] {'bl','dir'}, use_global_device_ids=true, to_apply=%region_8.9 | all-reduce | flops 6144 | bytes 49152 | tf_op jit(solution)/shard_map/while/body/eval_jaxpr/while/body/eval_jaxpr/psum | solution.py:125
  1453.3 101.4 %psum.29 = f32[12,512]{0,1:T(8,128)S(1)} all-reduce(f32[12,512]{0,1:T(8,128)S(1)} %add_bitcast_fusion.2), channel_id=1, replica_groups=mesh['bl'=32,'dir'=16] {'bl','dir'}, use_global_device_ids=true, to_apply=%region_8.9 | all-reduce | flops 6144 | bytes 49152 | tf_op jit(solution)/shard_map/while/body/eval_jaxpr/while/body/eval_jaxpr/psum | solution.py:125
  1561.2 2.3 fusion.153
  1563.6 6.7 copy.1417
  (794 shorter events, 130.7 us)
Async XLA Ops:
  7.2 98.3 %reduce-scatter.2.cloned.1.call-start = ((), (), s32[]{:S(2)}) async-start(), calls=%async_computation.1 | async-start | bytes 139264 | tf_op jit(solution)/shard_map/reduce_scatter | solution.py:97
  45.5 1.8 copy-start.3
  45.6 1.8 copy-start.4
  45.6 1.8 copy-start.5
  45.6 1.8 copy-start.6
  48.4 57.1 %copy-start.8 = (f32[8,1,256]{2,1,0:T(1,128)S(1)}, f32[8,1,256]{2,1,0:T(1,128)}, u32[]{:S(2)}) copy-start(f32[8,1,256]{2,1,0:T(1,128)} %param.21) | copy-start | bytes 24580
  48.4 57.8 %copy-start = (s32[2,256]{1,0:T(2,128)S(1)}, s32[2,256]{1,0:T(2,128)}, u32[]{:S(2)}) copy-start(s32[2,256]{1,0:T(2,128)} %param.24) | copy-start | bytes 6148
  48.4 57.8 %copy-start.1 = (bf16[2,8,16,256]{3,2,1,0:T(8,128)(2,1)S(1)}, bf16[2,8,16,256]{3,2,1,0:T(8,128)(2,1)}, u32[]{:S(2)}) copy-start(bf16[2,8,16,256]{3,2,1,0:T(8,128)(2,1)} %param.22) | copy-start | bytes 393220
  48.4 57.8 %copy-start.7 = (s32[3]{0:T(128)S(1)}, s32[3]{0:T(128)}, u32[]{:S(2)}) copy-start(s32[3]{0:T(128)} %constant.291.clone.1) | copy-start | bytes 40
  48.4 57.8 %copy-start.9 = (s32[32]{0:T(128)S(1)}, s32[32]{0:T(128)}, u32[]{:S(2)}) copy-start(s32[32]{0:T(128)} %param.25) | copy-start | bytes 388
  48.5 57.8 %copy-start.10 = (s32[32]{0:T(128)S(1)}, s32[32]{0:T(128)}, u32[]{:S(2)}) copy-start(s32[32]{0:T(128)} %param.27) | copy-start | bytes 388
  48.5 57.8 %copy-start.11 = (s32[32]{0:T(128)S(1)}, s32[32]{0:T(128)}, u32[]{:S(2)}) copy-start(s32[32]{0:T(128)} %param.26) | copy-start | bytes 388
  106.3 135.9 %all-reduce.2.cloned.1.call-start = ((), (), s32[]{:S(2)}) async-start(), calls=%async_computation.2 | async-start | bytes 131072 | tf_op jit(solution)/shard_map/while/body/eval_jaxpr/psum | solution.py:12
  482.8 119.7 %all-reduce.2.cloned.1.call-start = ((), (), s32[]{:S(2)}) async-start(), calls=%async_computation.2 | async-start | bytes 131072 | tf_op jit(solution)/shard_map/while/body/eval_jaxpr/psum | solution.py:12
  843.1 119.7 %all-reduce.2.cloned.1.call-start = ((), (), s32[]{:S(2)}) async-start(), calls=%async_computation.2 | async-start | bytes 131072 | tf_op jit(solution)/shard_map/while/body/eval_jaxpr/psum | solution.py:12
  1203.3 119.7 %all-reduce.2.cloned.1.call-start = ((), (), s32[]{:S(2)}) async-start(), calls=%async_computation.2 | async-start | bytes 131072 | tf_op jit(solution)/shard_map/while/body/eval_jaxpr/psum | solution.py:12
  1563.6 6.7 copy-start.2
Sparse Core Ops, SparseCore 0:
  48.5 56.9 reduce-scatter.1
  110.4 131.8 all-reduce.1
  486.8 115.5 all-reduce.1
  847.1 115.5 all-reduce.1
  1207.3 115.5 all-reduce.1
where the time goes:
time: 1580 us
  blocking collectives  884 us (56%)
  waiting for transfers between devices  502 us (32%)
  local copies, waits for them, and re-layouts  93.9 us (6%)
  other arithmetic  57.8 us (4%)
  loops' own time  25.7 us (2%)
    psum x8, blocking collectives, iterate(): gathered_sums = lax.psum(local_sums, ('bl', 'dir'))  854 us
    psum x4, waiting for transfers between devices, from_root(): return lax.psum(jnp.where(mine, shard, jnp.zeros_like(shard)), axis)  453 us
    reduce_scatter x1, waiting for transfers between devices, on_device(): lax.psum_scatter(partial_value, 'dir', scatter_dimension=1, tiled=True)  49.5 us
  transfers between devices with their start and end apart: 5, of which 5 were waited for; matrix products, arithmetic and copies ran while one was open for 2% of the time, Pallas kernels for 0%

commit v1 on v0

--- a/solution.py
+++ b/solution.py
@@ -5,6 +5,12 @@
 
 LM_ITERS = 2
 SOLVED = 4
+
+
+def gather_and_add(x, name):
+    pieces = lax.all_gather(x, name, axis=0, tiled=False)
+    total = pieces.sum(axis=0)
+    return total
 
 
 def from_root(shard, axis, root):
@@ -122,7 +128,7 @@
                 jax.ops.segment_sum(leading_endpoint.T, stations[0], station_count)
                 + jax.ops.segment_sum(second.T, stations[1], station_count)
             ).T
-            gathered_sums = lax.psum(local_sums, ("bl", "dir"))
+            gathered_sums = gather_and_add(local_sums, ("bl", "dir"))
             updated = solve_station(gathered_sums, gain_now, damp_value)
             return jnp.where(round_index < counts[which], updated, gain_now)
 

time: 1580 us -> 2520 us (1.59)
  waiting for transfers between devices: 502 us -> 2270 us
  blocking collectives: 884 us -> 29.8 us
  other arithmetic: 57.8 us -> 107 us
    all_gather x0 -> x8, waiting for transfers between devices: none -> 1760 us  [gather_and_add(): pieces = lax.all_gather(x, name, axis=0, tiled=False)]
    psum x8 -> x0, blocking collectives: 854 us -> none  [iterate(): gathered_sums = lax.psum(local_sums, ('bl', 'dir'))]
    reduce_sum x0 -> x8, other arithmetic: none -> 53.9 us  [gather_and_add(): total = pieces.sum(axis=0)]
  transfers between devices with their start and end apart: 5 -> 13, of which waited for: 5 -> 13; matrix products, arithmetic and copies ran while one was open for 2% -> 1% of each run, Pallas kernels for 0% -> 0%
where the time goes in v1:
time: 2520 us
  waiting for transfers between devices  2270 us (90%)
  other arithmetic  107 us (4%)
  local copies, waits for them, and re-layouts  69 us (3%)
  blocking collectives  29.8 us (1%)
  loops' own time  25.5 us (1%)
    all_gather x8, waiting for transfers between devices, gather_and_add(): pieces = lax.all_gather(x, name, axis=0, tiled=False)  1760 us
    psum x4, waiting for transfers between devices, from_root(): return lax.psum(jnp.where(mine, shard, jnp.zeros_like(shard)), axis)  459 us
    reduce_sum x8, other arithmetic, gather_and_add(): total = pieces.sum(axis=0)  53.9 us
  transfers between devices with their start and end apart: 13, of which 13 were waited for; matrix products, arithmetic and copies ran while one was open for 1% of the time, Pallas kernels for 0%

profile of v1, /device:TPU:1, one launch (start us, length us, event | category | flops | bytes accessed | tf_op | source)
XLA Modules:
  0.0 2519.3 jit_solution(11574973723410222921)
XLA Ops:
  9.8 29.8 %all_gather.19 = f32[32,8,512]{0,1,2:T(8,128)S(1)} all-gather(f32[32,8,16]{0,1,2:T(8,128)S(1)} %copy.860), channel_id=1, replica_groups=mesh['bl'=32,'dir'=16] {'bl'}, dimensions={2}, use_global_device_ids=true | all-gather | bytes 540672 | tf_op jit(solution)/shard_map/all_gather | solution.py:87
  48.5 7.4 copy.872
  55.9 49.6 %reduce-scatter.2.cloned.1.call-done = f32[8,1,256]{2,0,1:T(8,128)} async-done(((f32[8,16,256]{2,0,1:T(8,128)}), f32[8,1,256]{2,0,1:T(8,128)}) %reduce-scatter.2.cloned.1.call-update) | async-done | bytes 8208 | tf_op jit(solution)/shard_map/reduce_scatter | solution.py:103
  106.3 2399.1 %while.54 = (s32[]{:T(128)}, f32[32,8,512]{1,2,0:T(8,128)}, f32[8,1,256]{2,1,0:T(1,128)S(1)}, s32[32]{0:T(128)S(1)}, bf16[2,8,16,256]{3,2,1,0:T(8,128)(2,1)S(1)}...) while((s32[]{:T(128)}, f32[32,8,512]{1,2,0:T(8,128)}, ...), condition=%wide.region_10.13_spmd, body=%wide.region_2.12_spmd.sunk | while | flops 3456559 | bytes 57476556 | solution.py:139
  116.8 125.4 %all-reduce.2.cloned.1.call-done = bf16[8,16,256]{2,1,0:T(8,128)(2,1)} async-done(((bf16[8,16,256]{2,1,0:T(8,128)(2,1)}), bf16[8,16,256]{2,1,0:T(8,128)(2,1)}) %all-reduce.2.cloned.1.call-update) | async-done | bytes 65552 | tf_op jit(solution)/shard_map/while/body/eval_jaxpr/psum | solution.py:18
  243.2 469.6 %while.55 = (s32[]{:T(128)}, f32[8,512]{0,1:T(8,128)S(1)}, s32[1]{0:T(128)}, s32[2,256]{1,0:T(2,128)S(1)}, f32[8,1,256]{2,1,0:T(1,128)S(1)}, /*index=5*/f32[8,1,...) while((s32[]{:T(128)}, f32[8,512]{0,1:T(8,128)S(1)}, ...), condition=%wide.region_9.11_spmd, body=%wide.region_5.10_spmd.sunk | while | flops 3298305 | bytes 55879916 | solution.py:135
  250.2 226.5 %all-gather.6.cloned.1.call-done = f32[512,12,512]{2,1,0:T(8,128)} async-done(((f32[1,12,512]{2,1,0:T(8,128)}), f32[512,12,512]{2,1,0:T(8,128)}) %all-gather.6.cloned.1.call-update) | async-done | bytes 12582928 | tf_op jit(solution)/shard_map/while/body/eval_jaxpr/while/body/eval_jaxpr/all_gather | solution.py:11
  490.9 214.8 %all-gather.6.cloned.1.call-done = f32[512,12,512]{2,1,0:T(8,128)} async-done(((f32[1,12,512]{2,1,0:T(8,128)}), f32[512,12,512]{2,1,0:T(8,128)}) %all-gather.6.cloned.1.call-update) | async-done | bytes 12582928 | tf_op jit(solution)/shard_map/while/body/eval_jaxpr/while/body/eval_jaxpr/all_gather | solution.py:11
  705.6 6.7 reduce_sum.41
  727.3 111.0 %all-reduce.2.cloned.1.call-done = bf16[8,16,256]{2,1,0:T(8,128)(2,1)} async-done(((bf16[8,16,256]{2,1,0:T(8,128)(2,1)}), bf16[8,16,256]{2,1,0:T(8,128)(2,1)}) %all-reduce.2.cloned.1.call-update) | async-done | bytes 65552 | tf_op jit(solution)/shard_map/while/body/eval_jaxpr/psum | solution.py:18
  839.4 469.6 %while.55 = (s32[]{:T(128)}, f32[8,512]{0,1:T(8,128)S(1)}, s32[1]{0:T(128)}, s32[2,256]{1,0:T(2,128)S(1)}, f32[8,1,256]{2,1,0:T(1,128)S(1)}, /*index=5*/f32[8,1,...) while((s32[]{:T(128)}, f32[8,512]{0,1:T(8,128)S(1)}, ...), condition=%wide.region_9.11_spmd, body=%wide.region_5.10_spmd.sunk | while | flops 3298305 | bytes 55879916 | solution.py:135
  846.4 226.5 %all-gather.6.cloned.1.call-done = f32[512,12,512]{2,1,0:T(8,128)} async-done(((f32[1,12,512]{2,1,0:T(8,128)}), f32[512,12,512]{2,1,0:T(8,128)}) %all-gather.6.cloned.1.call-update) | async-done | bytes 12582928 | tf_op jit(solution)/shard_map/while/body/eval_jaxpr/while/body/eval_jaxpr/all_gather | solution.py:11
  1087.0 214.8 %all-gather.6.cloned.1.call-done = f32[512,12,512]{2,1,0:T(8,128)} async-done(((f32[1,12,512]{2,1,0:T(8,128)}), f32[512,12,512]{2,1,0:T(8,128)}) %all-gather.6.cloned.1.call-update) | async-done | bytes 12582928 | tf_op jit(solution)/shard_map/while/body/eval_jaxpr/while/body/eval_jaxpr/all_gather | solution.py:11
  1323.5 111.0 %all-reduce.2.cloned.1.call-done = bf16[8,16,256]{2,1,0:T(8,128)(2,1)} async-done(((bf16[8,16,256]{2,1,0:T(8,128)(2,1)}), bf16[8,16,256]{2,1,0:T(8,128)(2,1)}) %all-reduce.2.cloned.1.call-update) | async-done | bytes 65552 | tf_op jit(solution)/shard_map/while/body/eval_jaxpr/psum | solution.py:18
  1435.5 469.6 %while.55 = (s32[]{:T(128)}, f32[8,512]{0,1:T(8,128)S(1)}, s32[1]{0:T(128)}, s32[2,256]{1,0:T(2,128)S(1)}, f32[8,1,256]{2,1,0:T(1,128)S(1)}, /*index=5*/f32[8,1,...) while((s32[]{:T(128)}, f32[8,512]{0,1:T(8,128)S(1)}, ...), condition=%wide.region_9.11_spmd, body=%wide.region_5.10_spmd.sunk | while | flops 3298305 | bytes 55879916 | solution.py:135
  1442.5 226.5 %all-gather.6.cloned.1.call-done = f32[512,12,512]{2,1,0:T(8,128)} async-done(((f32[1,12,512]{2,1,0:T(8,128)}), f32[512,12,512]{2,1,0:T(8,128)}) %all-gather.6.cloned.1.call-update) | async-done | bytes 12582928 | tf_op jit(solution)/shard_map/while/body/eval_jaxpr/while/body/eval_jaxpr/all_gather | solution.py:11
  1669.0 6.7 reduce_sum.41
  1683.2 214.8 %all-gather.6.cloned.1.call-done = f32[512,12,512]{2,1,0:T(8,128)} async-done(((f32[1,12,512]{2,1,0:T(8,128)}), f32[512,12,512]{2,1,0:T(8,128)}) %all-gather.6.cloned.1.call-update) | async-done | bytes 12582928 | tf_op jit(solution)/shard_map/while/body/eval_jaxpr/while/body/eval_jaxpr/all_gather | solution.py:11
  1898.0 6.7 reduce_sum.41
  1919.7 111.0 %all-reduce.2.cloned.1.call-done = bf16[8,16,256]{2,1,0:T(8,128)(2,1)} async-done(((bf16[8,16,256]{2,1,0:T(8,128)(2,1)}), bf16[8,16,256]{2,1,0:T(8,128)(2,1)}) %all-reduce.2.cloned.1.call-update) | async-done | bytes 65552 | tf_op jit(solution)/shard_map/while/body/eval_jaxpr/psum | solution.py:18
  2031.7 469.6 %while.55 = (s32[]{:T(128)}, f32[8,512]{0,1:T(8,128)S(1)}, s32[1]{0:T(128)}, s32[2,256]{1,0:T(2,128)S(1)}, f32[8,1,256]{2,1,0:T(1,128)S(1)}, /*index=5*/f32[8,1,...) while((s32[]{:T(128)}, f32[8,512]{0,1:T(8,128)S(1)}, ...), condition=%wide.region_9.11_spmd, body=%wide.region_5.10_spmd.sunk | while | flops 3298305 | bytes 55879916 | solution.py:135
  2038.7 226.5 %all-gather.6.cloned.1.call-done = f32[512,12,512]{2,1,0:T(8,128)} async-done(((f32[1,12,512]{2,1,0:T(8,128)}), f32[512,12,512]{2,1,0:T(8,128)}) %all-gather.6.cloned.1.call-update) | async-done | bytes 12582928 | tf_op jit(solution)/shard_map/while/body/eval_jaxpr/while/body/eval_jaxpr/all_gather | solution.py:11
  2279.4 214.8 %all-gather.6.cloned.1.call-done = f32[512,12,512]{2,1,0:T(8,128)} async-done(((f32[1,12,512]{2,1,0:T(8,128)}), f32[512,12,512]{2,1,0:T(8,128)}) %all-gather.6.cloned.1.call-update) | async-done | bytes 12582928 | tf_op jit(solution)/shard_map/while/body/eval_jaxpr/while/body/eval_jaxpr/all_gather | solution.py:11
  2494.1 6.7 reduce_sum.41
  (706 shorter events, 142.6 us)
Async XLA Ops:
  7.2 98.3 %reduce-scatter.2.cloned.1.call-start = ((), (), s32[]{:S(2)}) async-start(), calls=%async_computation.1 | async-start | bytes 139264 | tf_op jit(solution)/shard_map/reduce_scatter | solution.py:103
  45.5 1.8 copy-start.3
  45.6 1.8 copy-start.4
  45.6 1.8 copy-start.5
  48.4 57.1 %copy-start.8 = (f32[8,1,256]{2,1,0:T(1,128)S(1)}, f32[8,1,256]{2,1,0:T(1,128)}, u32[]{:S(2)}) copy-start(f32[8,1,256]{2,1,0:T(1,128)} %param.21) | copy-start | bytes 24580
  48.4 57.8 %copy-start = (s32[2,256]{1,0:T(2,128)S(1)}, s32[2,256]{1,0:T(2,128)}, u32[]{:S(2)}) copy-start(s32[2,256]{1,0:T(2,128)} %param.24) | copy-start | bytes 6148
  48.4 57.8 %copy-start.1 = (bf16[2,8,16,256]{3,2,1,0:T(8,128)(2,1)S(1)}, bf16[2,8,16,256]{3,2,1,0:T(8,128)(2,1)}, u32[]{:S(2)}) copy-start(bf16[2,8,16,256]{3,2,1,0:T(8,128)(2,1)} %param.22) | copy-start | bytes 393220
  48.4 57.8 %copy-start.7 = (s32[3]{0:T(128)S(1)}, s32[3]{0:T(128)}, u32[]{:S(2)}) copy-start(s32[3]{0:T(128)} %constant.291.clone.1) | copy-start | bytes 40
  48.4 57.8 %copy-start.9 = (s32[32]{0:T(128)S(1)}, s32[32]{0:T(128)}, u32[]{:S(2)}) copy-start(s32[32]{0:T(128)} %param.25) | copy-start | bytes 388
  48.5 57.8 %copy-start.10 = (s32[32]{0:T(128)S(1)}, s32[32]{0:T(128)}, u32[]{:S(2)}) copy-start(s32[32]{0:T(128)} %param.27) | copy-start | bytes 388
  48.5 57.8 %copy-start.11 = (s32[32]{0:T(128)S(1)}, s32[32]{0:T(128)}, u32[]{:S(2)}) copy-start(s32[32]{0:T(128)} %param.26) | copy-start | bytes 388
  106.3 135.9 %all-reduce.2.cloned.1.call-start = ((), (), s32[]{:S(2)}) async-start(), calls=%async_computation.2 | async-start | bytes 131072 | tf_op jit(solution)/shard_map/while/body/eval_jaxpr/psum | solution.py:18
  243.2 233.5 %all-gather.6.cloned.1.call-start = ((), (), s32[]{:S(2)}) async-start(), calls=%async_computation.3 | async-start | bytes 16809984 | tf_op jit(solution)/shard_map/while/body/eval_jaxpr/while/body/eval_jaxpr/all_gather | solution.py:11
  483.9 221.8 %all-gather.6.cloned.1.call-start = ((), (), s32[]{:S(2)}) async-start(), calls=%async_computation.3 | async-start | bytes 16809984 | tf_op jit(solution)/shard_map/while/body/eval_jaxpr/while/body/eval_jaxpr/all_gather | solution.py:11
  716.9 121.4 %all-reduce.2.cloned.1.call-start = ((), (), s32[]{:S(2)}) async-start(), calls=%async_computation.2 | async-start | bytes 131072 | tf_op jit(solution)/shard_map/while/body/eval_jaxpr/psum | solution.py:18
  839.4 233.5 %all-gather.6.cloned.1.call-start = ((), (), s32[]{:S(2)}) async-start(), calls=%async_computation.3 | async-start | bytes 16809984 | tf_op jit(solution)/shard_map/while/body/eval_jaxpr/while/body/eval_jaxpr/all_gather | solution.py:11
  1080.0 221.8 %all-gather.6.cloned.1.call-start = ((), (), s32[]{:S(2)}) async-start(), calls=%async_computation.3 | async-start | bytes 16809984 | tf_op jit(solution)/shard_map/while/body/eval_jaxpr/while/body/eval_jaxpr/all_gather | solution.py:11
  1313.1 121.4 %all-reduce.2.cloned.1.call-start = ((), (), s32[]{:S(2)}) async-start(), calls=%async_computation.2 | async-start | bytes 131072 | tf_op jit(solution)/shard_map/while/body/eval_jaxpr/psum | solution.py:18
  1435.5 233.5 %all-gather.6.cloned.1.call-start = ((), (), s32[]{:S(2)}) async-start(), calls=%async_computation.3 | async-start | bytes 16809984 | tf_op jit(solution)/shard_map/while/body/eval_jaxpr/while/body/eval_jaxpr/all_gather | solution.py:11
  1676.2 221.8 %all-gather.6.cloned.1.call-start = ((), (), s32[]{:S(2)}) async-start(), calls=%async_computation.3 | async-start | bytes 16809984 | tf_op jit(solution)/shard_map/while/body/eval_jaxpr/while/body/eval_jaxpr/all_gather | solution.py:11
  1909.3 121.4 %all-reduce.2.cloned.1.call-start = ((), (), s32[]{:S(2)}) async-start(), calls=%async_computation.2 | async-start | bytes 131072 | tf_op jit(solution)/shard_map/while/body/eval_jaxpr/psum | solution.py:18
  2031.7 233.5 %all-gather.6.cloned.1.call-start = ((), (), s32[]{:S(2)}) async-start(), calls=%async_computation.3 | async-start | bytes 16809984 | tf_op jit(solution)/shard_map/while/body/eval_jaxpr/while/body/eval_jaxpr/all_gather | solution.py:11
  2272.4 221.8 %all-gather.6.cloned.1.call-start = ((), (), s32[]{:S(2)}) async-start(), calls=%async_computation.3 | async-start | bytes 16809984 | tf_op jit(solution)/shard_map/while/body/eval_jaxpr/while/body/eval_jaxpr/all_gather | solution.py:11
  2505.4 6.7 copy-start.2
  (1 other events, 1.8 us)
Sparse Core Ops, SparseCore 0:
  48.5 56.9 reduce-scatter.1
  110.3 131.8 all-reduce.1
  249.6 227.0 all-gather.5
  490.3 215.3 all-gather.5
  720.9 117.4 all-reduce.1
  845.8 227.0 all-gather.5
  1086.4 215.3 all-gather.5
  1317.1 117.4 all-reduce.1
  1441.9 227.0 all-gather.5
  1682.6 215.3 all-gather.5
  1913.2 117.4 all-reduce.1
  2038.1 227.0 all-gather.5
  2278.7 215.3 all-gather.5
